TPU v7x, 256 devices: a whole 4x4x8 slice. The times are simulated.
256 devices in a mesh: row: 16 (over x, y), col: 16 (over z, core).
Axes of the slice: x: 4, y: 4, z: 8, core: 2. Of those that a mesh axis runs over, the one named last changes fastest.
Arguments:
- start_block: float32 [65536, 128], P(('row', 'col')), may hold values from -6 to 6
- vertex_scale: float32 [65536], P(('row', 'col')), may hold values from 0.015625 to 0.0625
- adj_tiles: bfloat16 [16, 16, 64, 128, 128], P('row', 'col'), may hold values from 0 to 1
- tile_row: int32 [16, 16, 64], P('row', 'col'), may hold values from 0 to 31
- tile_col: int32 [16, 16, 64], P('row', 'col'), may hold values from 0 to 31
- live_count: int32 [16, 16], P('row', 'col'), may hold values from 16 to 64, as said below
- rotation_first: float32 [256, 128], replicated, may hold values from -0.375 to 0.375
- rotation_second: float32 [384, 128], replicated, may hold values from -0.3125 to 0.3125
Outputs:
- final_block: float32 [65536, 128], P(('row', 'col'))
- final_image: float32 [65536, 128], P(('row', 'col'))
Inputs may be any that keep to these rules, and one draw needn't show every extreme that they name: Slots from live_count on are ignored; at least one device has all 64 slots live in every draw.
All inputs are finite; a program needn't handle non-finite values.
Results may differ from a plain program's by a relative error of at most 0.01.
Values may be sent and summed in bfloat16 or wider, within the bound.
A program may use at most 64 MiB of HBM per device.

v0:
```python
import jax
import jax.numpy as jnp
from jax import lax
from jax.sharding import PartitionSpec as P

HIGH = lax.Precision.HIGHEST


def tile_products(tiles_here, cols_here, count_here, flat_panel, span_slots, tile_side, width_k):
    alive_mask = jnp.arange(span_slots, dtype=jnp.int32) < count_here
    pieces = jnp.take(flat_panel, cols_here, axis=0)
    pieces = jnp.where(alive_mask[:, None], pieces, jnp.zeros_like(pieces))
    pieces = pieces.reshape(span_slots, tile_side, width_k)
    tile_out = jnp.einsum("tab,tbk->tak", tiles_here, pieces, preferred_element_type=jnp.float32)
    return tile_out.reshape(span_slots, tile_side * width_k)


def place_rows(rows_slot, tile_out, row_tiles, tile_side, width_k):
    placed = jax.ops.segment_sum(tile_out, rows_slot, num_segments=row_tiles)
    return placed.reshape(row_tiles * tile_side, width_k)


def apply_operator(block, vertex_scale, tiles_here, rows_here, cols_here, count_here):
    tile_side = tiles_here.shape[-1]
    width_k = block.shape[1]
    slot_total = tiles_here.shape[0]
    scaled = (vertex_scale[:, None] * block).astype(jnp.bfloat16)
    gathered = lax.all_gather(scaled, "col", axis=0, tiled=True)
    flat_panel = gathered.reshape(gathered.shape[0] // tile_side, tile_side * width_k)
    row_tiles = lax.axis_size("row") * block.shape[0] // tile_side
    tile_out = tile_products(
        tiles_here, cols_here, count_here, flat_panel, slot_total, tile_side, width_k
    )
    partial_value = place_rows(rows_here, tile_out, row_tiles, tile_side, width_k)
    summed = lax.psum_scatter(
        partial_value.astype(jnp.bfloat16), "row", scatter_dimension=0, tiled=True
    ).astype(jnp.float32)
    return block - vertex_scale[:, None] * summed


def inner(left, right):
    return jnp.einsum("sk,sl->kl", left, right, precision=HIGH)


def residual_block(block, image, verts_all):
    gram = lax.psum(inner(block, image), ("row", "col")) / verts_all
    resid = image - jnp.dot(block, gram, precision=HIGH)
    colsq = lax.psum(jnp.sum(resid * resid, axis=0), ("row", "col"))
    return resid * lax.rsqrt(colsq / verts_all + 1e-06)


def local(
    start_block,
    vertex_scale,
    adj_tiles,
    tile_row,
    tile_col,
    live_count,
    rotation_first,
    rotation_second,
):
    width_k = start_block.shape[1]
    verts_all = start_block.shape[0] * lax.axis_size("row") * lax.axis_size("col")
    tiles_here = adj_tiles[0, 0]
    rows_here = tile_row[0, 0]
    cols_here = tile_col[0, 0]
    count_here = live_count[0, 0]

    def oper(block):
        return apply_operator(block, vertex_scale, tiles_here, rows_here, cols_here, count_here)

    image0 = oper(start_block)
    search0 = residual_block(start_block, image0, verts_all)
    simage0 = oper(search0)
    rot_x, rot_w = (rotation_first[:width_k], rotation_first[width_k:])
    block1 = jnp.dot(start_block, rot_x, precision=HIGH) + jnp.dot(search0, rot_w, precision=HIGH)
    image1 = jnp.dot(image0, rot_x, precision=HIGH) + jnp.dot(simage0, rot_w, precision=HIGH)
    prev1 = jnp.dot(search0, rot_w, precision=HIGH)
    pimage1 = jnp.dot(simage0, rot_w, precision=HIGH)
    search1 = residual_block(block1, image1, verts_all)
    simage1 = oper(search1)
    rot_qx = rotation_second[:width_k]
    rot_qw = rotation_second[width_k : 2 * width_k]
    rot_qp = rotation_second[2 * width_k :]
    final_block = (
        jnp.dot(block1, rot_qx, precision=HIGH)
        + jnp.dot(search1, rot_qw, precision=HIGH)
        + jnp.dot(prev1, rot_qp, precision=HIGH)
    )
    final_image = (
        jnp.dot(image1, rot_qx, precision=HIGH)
        + jnp.dot(simage1, rot_qw, precision=HIGH)
        + jnp.dot(pimage1, rot_qp, precision=HIGH)
    )
    return (final_block, final_image)


def solution(mesh):
    placed = (
        P(("row", "col"), None),
        P(("row", "col")),
        P("row", "col", None, None, None),
        P("row", "col", None),
        P("row", "col", None),
        P("row", "col"),
        P(),
        P(),
    )
    return jax.shard_map(
        local,
        mesh=mesh,
        in_specs=placed,
        out_specs=(P(("row", "col"), None), P(("row", "col"), None)),
        check_vma=False,
    )
```

profile of v0, /device:TPU:2, one launch (start us, length us, event | category | flops | bytes accessed | tf_op | source)
XLA Modules:
  0.0 1100.4 jit_solution(16218495195349804594)
XLA Ops:
  11.7 39.2 %all-gather.4.cloned.1.call-done = bf16[4096,128]{0,1:T(8,128)(2,1)} async-done(((bf16[256,128]{0,1:T(8,128)(2,1)}), bf16[4096,128]{0,1:T(8,128)(2,1)}) %all-gather.4.cloned.1.call-update) | async-done | bytes 1048592 | tf_op jit(solution)/shard_map/all_gather | solution.py:28
  51.0 2.3 copy.19
  54.8 3.2 gather_fusion
  58.0 1.9 fusion.14
  60.5 3.6 convolution_bitcast_fusion.2
  64.0 5.6 copy.21
  69.6 10.6 scatter_custom_fusion
  83.3 2.3 copy.22
  85.6 76.8 %reduce-scatter.4.cloned.1.call-done = bf16[256,128]{0,1:T(8,128)(2,1)} async-done(((bf16[4096,128]{0,1:T(8,128)(2,1)}), bf16[256,128]{0,1:T(8,128)(2,1)}) %reduce-scatter.4.cloned.1.call-update) | async-done | bytes 65552 | tf_op jit(solution)/shard_map/reduce_scatter | solution.py:35
  162.4 1.7 convolution_bitcast_fusion.4
  164.3 241.9 %all-reduce.3.cloned.1.call-done = f32[128,128]{0,1:T(8,128)} async-done(((f32[128,128]{0,1:T(8,128)}), f32[128,128]{0,1:T(8,128)}) %all-reduce.3.cloned.1.call-update) | async-done | bytes 65552 | tf_op jit(solution)/shard_map/psum | solution.py:46
  407.4 74.2 %psum.29 = f32[128]{0:T(128)S(1)} all-reduce(f32[128]{0:T(128)S(1)} %get-tuple-element.3), channel_id=1, replica_groups=mesh['row'=16,'col'=16] {'row','col'}, use_global_device_ids=true, to_apply=%region_4.6 | all-reduce | flops 128 | bytes 1024 | tf_op jit(solution)/shard_map/psum | solution.py:48
  483.1 33.3 %all-gather.6.cloned.1.call-done = bf16[4096,128]{0,1:T(8,128)(2,1)} async-done(((bf16[256,128]{0,1:T(8,128)(2,1)}), bf16[4096,128]{0,1:T(8,128)(2,1)}) %all-gather.6.cloned.1.call-update) | async-done | bytes 1048592 | tf_op jit(solution)/shard_map/all_gather | solution.py:28
  516.4 2.3 copy.24
  520.2 3.2 gather_fusion.1
  523.4 1.9 fusion.13
  525.9 3.6 convolution_bitcast_fusion.1
  529.5 5.6 copy.26
  535.1 10.6 scatter_custom_fusion.1
  548.7 2.3 copy.27
  552.1 75.8 %reduce-scatter.6.cloned.1.call-done = bf16[256,128]{0,1:T(8,128)(2,1)} async-done(((bf16[4096,128]{0,1:T(8,128)(2,1)}), bf16[256,128]{0,1:T(8,128)(2,1)}) %reduce-scatter.6.cloned.1.call-update) | async-done | bytes 65552 | tf_op jit(solution)/shard_map/reduce_scatter | solution.py:35
  631.2 238.6 %all-reduce.5.cloned.1.call-done = f32[128,128]{0,1:T(8,128)} async-done(((f32[128,128]{0,1:T(8,128)}), f32[128,128]{0,1:T(8,128)}) %all-reduce.5.cloned.1.call-update) | async-done | bytes 65552 | tf_op jit(solution)/shard_map/psum | solution.py:46
  871.0 74.2 %psum.31 = f32[128]{0:T(128)S(1)} all-reduce(f32[128]{0:T(128)S(1)} %get-tuple-element.5), channel_id=1, replica_groups=mesh['row'=16,'col'=16] {'row','col'}, use_global_device_ids=true, to_apply=%region_9.11 | all-reduce | flops 128 | bytes 1024 | tf_op jit(solution)/shard_map/psum | solution.py:48
  946.0 33.5 %all-gather.8.cloned.1.call-done = bf16[4096,128]{0,1:T(8,128)(2,1)} async-done(((bf16[256,128]{0,1:T(8,128)(2,1)}), bf16[4096,128]{0,1:T(8,128)(2,1)}) %all-gather.8.cloned.1.call-update) | async-done | bytes 1048592 | tf_op jit(solution)/shard_map/all_gather | solution.py:28
  979.5 2.3 copy.31
  983.3 3.2 gather_fusion.2
  986.5 1.9 fusion.12
  989.0 3.6 convolution_bitcast_fusion
  992.6 5.6 copy.33
  998.2 10.6 scatter_custom_fusion.2
  1011.8 2.3 copy.34
  1016.2 74.7 %reduce-scatter.8.cloned.1.call-done = bf16[256,128]{0,1:T(8,128)(2,1)} async-done(((bf16[4096,128]{0,1:T(8,128)(2,1)}), bf16[256,128]{0,1:T(8,128)(2,1)}) %reduce-scatter.8.cloned.1.call-update) | async-done | bytes 65552 | tf_op jit(solution)/shard_map/reduce_scatter | solution.py:35
  (79 shorter events, 32.5 us)
Async XLA Ops:
  7.2 53.3 %copy-start = (bf16[1,1,64,128,128]{4,3,2,1,0:T(8,128)(2,1)S(1)}, bf16[1,1,64,128,128]{4,3,2,1,0:T(8,128)(2,1)}, u32[]{:S(2)}) copy-start(bf16[1,1,64,128,128]{4,3,2,1,0:T(8,128)(2,1)} %param.12) | copy-start | bytes 6291460
  7.2 43.8 %all-gather.4.cloned.1.call-start = ((), (), s32[]{:S(2)}) async-start(), calls=%async_computation.3 | async-start | bytes 1114112 | tf_op jit(solution)/shard_map/all_gather | solution.py:28
  9.7 152.7 %reduce-scatter.4.cloned.1.call-start = ((), (), s32[]{:S(2)}) async-start(), calls=%async_computation.4 | async-start | bytes 1114112 | tf_op jit(solution)/shard_map/reduce_scatter | solution.py:35
  83.3 79.2 %copy-start.1 = (f32[256,128]{1,0:T(8,128)S(1)}, f32[256,128]{1,0:T(8,128)}, u32[]{:S(2)}) copy-start(f32[256,128]{1,0:T(8,128)} %param.10) | copy-start | bytes 393220
  83.3 79.2 %copy-start.11 = (f32[256]{0:T(256)S(1)}, f32[256]{0:T(256)}, u32[]{:S(2)}) copy-start(f32[256]{0:T(256)} %param.11) | copy-start | bytes 3076
  85.6 320.6 %all-reduce.3.cloned.1.call-start = ((), (), s32[]{:S(2)}) async-start(), calls=%async_computation.5 | async-start | bytes 131072 | tf_op jit(solution)/shard_map/psum | solution.py:46
  164.2 352.2 %all-gather.6.cloned.1.call-start = ((), (), s32[]{:S(2)}) async-start(), calls=%async_computation.6 | async-start | bytes 1114112 | tf_op jit(solution)/shard_map/all_gather | solution.py:28
  481.6 0.5 copy-start.12
  482.9 145.0 %reduce-scatter.6.cloned.1.call-start = ((), (), s32[]{:S(2)}) async-start(), calls=%async_computation.7 | async-start | bytes 1114112 | tf_op jit(solution)/shard_map/reduce_scatter | solution.py:35
  548.7 2.6 copy-start.10
  548.7 2.6 copy-start.13
  548.7 81.2 %copy-start.9 = (bf16[256,128]{0,1:T(8,128)(2,1)S(1)}, bf16[256,128]{0,1:T(8,128)(2,1)}, u32[]{:S(2)}) copy-start(bf16[256,128]{0,1:T(8,128)(2,1)} %reduce-scatter.4.cloned.1.call-done) | copy-start | bytes 196612
  551.0 318.8 %all-reduce.5.cloned.1.call-start = ((), (), s32[]{:S(2)}) async-start(), calls=%async_computation.8 | async-start | bytes 131072 | tf_op jit(solution)/shard_map/psum | solution.py:46
  551.8 427.7 %copy-start.4 = (f32[256,128]{1,0:T(8,128)}, f32[256,128]{1,0:T(8,128)S(1)}, u32[]{:S(2)}) copy-start(f32[256,128]{1,0:T(8,128)S(1)} %fusion.29) | copy-start | bytes 393220
  552.1 427.4 %copy-start.2 = (f32[256,128]{1,0:T(8,128)}, f32[256,128]{1,0:T(8,128)S(1)}, u32[]{:S(2)}) copy-start(f32[256,128]{1,0:T(8,128)S(1)} %convolution_add_fusion.5) | copy-start | bytes 393220
  629.2 0.6 copy-start.6
  631.2 348.3 %all-gather.8.cloned.1.call-start = ((), (), s32[]{:S(2)}) async-start(), calls=%async_computation.9 | async-start | bytes 1114112 | tf_op jit(solution)/shard_map/all_gather | solution.py:28
  945.9 145.0 %reduce-scatter.8.cloned.1.call-start = ((), (), s32[]{:S(2)}) async-start(), calls=%async_computation.10 | async-start | bytes 1114112 | tf_op jit(solution)/shard_map/reduce_scatter | solution.py:35
  1011.8 2.3 copy-start.3
  1011.8 2.4 copy-start.8
  1011.8 3.5 copy-start.5
  1014.1 78.1 %copy-start.7 = (f32[256,128]{1,0:T(8,128)S(1)}, f32[256,128]{1,0:T(8,128)}, u32[]{:S(2)}) copy-start(f32[256,128]{1,0:T(8,128)} %copy-done.6) | copy-start | bytes 393220
Sparse Core Ops, SparseCore 0:
  10.3 40.5 all-gather.3
  85.7 76.6 reduce-scatter.3
  169.4 236.6 all-reduce.2
  483.0 33.3 all-gather.5
  551.2 76.6 reduce-scatter.5
  633.3 236.4 all-reduce.4
  946.1 33.3 all-gather.7
  1014.2 76.6 reduce-scatter.7
where the time goes:
time: 1110 us; the launch traced here: 1100 us
  waiting for transfers between devices  814 us (73%)
  blocking collectives  148 us (13%)
  local copies, waits for them, and re-layouts  52.7 us (5%)
  other arithmetic  46.7 us (4%)
  matrix products  22.4 us (2%)
  between operations  15.4 us (1%)
    psum x2, waiting for transfers between devices, residual_block(): gram = lax.psum(inner(block, image), ('row', 'col')) / verts_all  480 us
    reduce_scatter x3, waiting for transfers between devices, apply_operator(): lax.psum_scatter(partial_value.astype(jnp.bfloat16), 'row', scatter_dimen...  227 us
    psum x2, blocking collectives, residual_block(): colsq = lax.psum(jnp.sum(resid * resid, axis=0), ('row', 'col'))  148 us
    all_gather x3, waiting for transfers between devices, apply_operator(): gathered = lax.all_gather(scaled, 'col', axis=0, tiled=True)  106 us
    scatter-add x3, other arithmetic, place_rows(): placed = jax.ops.segment_sum(tile_out, rows_slot, num_segments=row_tiles)  31.9 us
  transfers between devices with their start and end apart: 8, of which 8 were waited for; matrix products, arithmetic and copies ran while one was open for 0% of the time, Pallas kernels for 0%

commit v1 on v0

--- a/solution.py
+++ b/solution.py
@@ -1,9 +1,38 @@
+import functools
 import jax
 import jax.numpy as jnp
 from jax import lax
 from jax.sharding import PartitionSpec as P
 
 HIGH = lax.Precision.HIGHEST
+
+
+def points_serve(sheet, axis_id):
+    high = lax.axis_size(axis_id)
+    d_next, shaped, heard = (high, lax.axis_index(axis_id), sheet.shape[0])
+    new = range(d_next)
+    u1 = range(d_next)
+    frames = list(map(lambda i: (i, (i + 1) % d_next), new))
+    f_now = map(lambda i: (i, (i - 1) % d_next), u1)
+    carry = jnp.zeros((*sheet.shape[:0], d_next * heard, *sheet.shape[1:]), sheet.dtype)
+    carry = lax.dynamic_update_slice_in_dim(carry, sheet, shaped * heard, axis=0)
+    value_now = t_next = sheet
+    tray = list(f_now)
+    x_next = d_next // 2
+    for b in range(1, x_next + 1):
+        value_now = lax.ppermute(value_now, axis_name=axis_id, perm=frames)
+        carry = lax.dynamic_update_slice_in_dim(
+            carry, value_now, (shaped - b) % d_next * heard, axis=0
+        )
+        if b < d_next - x_next:
+            t_next = lax.ppermute(t_next, axis_name=axis_id, perm=tray)
+            carry = lax.dynamic_update_slice_in_dim(
+                carry, t_next, (shaped + b) % d_next * heard, axis=0
+            )
+    return carry
+
+
+teams_draw = functools.partial(points_serve, axis_id="col")
 
 
 def tile_products(tiles_here, cols_here, count_here, flat_panel, span_slots, tile_side, width_k):
@@ -25,7 +54,7 @@
     width_k = block.shape[1]
     slot_total = tiles_here.shape[0]
     scaled = (vertex_scale[:, None] * block).astype(jnp.bfloat16)
-    gathered = lax.all_gather(scaled, "col", axis=0, tiled=True)
+    gathered = teams_draw(scaled)
     flat_panel = gathered.reshape(gathered.shape[0] // tile_side, tile_side * width_k)
     row_tiles = lax.axis_size("row") * block.shape[0] // tile_side
     tile_out = tile_products(

time: 1110 us -> 1120 us (level)
  waiting for transfers between devices: 814 us -> 724 us
  starting transfers between devices: 0.72 us -> 65.1 us
  local copies, waits for them, and re-layouts: 52.7 us -> 85.1 us
    all_gather x3 -> x0, waiting for transfers between devices: 106 us -> none  [apply_operator(): gathered = lax.all_gather(scaled, 'col', axis=0, tiled=True)]
    ppermute x0 -> x45, starting transfers between devices: none -> 64.7 us  [the longest x21 64.3 us: points_serve(): t_next = lax.ppermute(t_next, axis_name=axis_id, perm=tray)]
    dynamic_update_slice x0 -> x48, local copies, waits for them, and re-layouts: none -> 30 us  [the longest x24 15.1 us: points_serve(): lax.dynamic_update_slice_in_dim(carry, value_now, (shaped - b) % d_next *...]
    ppermute x0 -> x45, waiting for transfers between devices: none -> 21.1 us  [the longest x24 21.1 us: points_serve(): value_now = lax.ppermute(value_now, axis_name=axis_id, perm=frames)]
  transfers between devices with their start and end apart: 8 -> 50, of which waited for: 8 -> 28; matrix products, arithmetic and copies ran while one was open for 0% -> 4% of each run, Pallas kernels for 0% -> 0%
where the time goes in v1:
time: 1120 us; the launch traced here: 1110 us
  waiting for transfers between devices  724 us (65%)
  blocking collectives  149 us (13%)
  local copies, waits for them, and re-layouts  85.1 us (8%)
  starting transfers between devices  65.1 us (6%)
  other arithmetic  45.5 us (4%)
  matrix products  22.5 us (2%)
  between operations  16 us (1%)
    psum x2, waiting for transfers between devices, residual_block(): gram = lax.psum(inner(block, image), ('row', 'col')) / verts_all  480 us
    reduce_scatter x3, waiting for transfers between devices, apply_operator(): lax.psum_scatter(partial_value.astype(jnp.bfloat16), 'row', scatter_dimen...  222 us
    psum x2, blocking collectives, residual_block(): colsq = lax.psum(jnp.sum(resid * resid, axis=0), ('row', 'col'))  149 us
    ppermute x21, starting transfers between devices, points_serve(): t_next = lax.ppermute(t_next, axis_name=axis_id, perm=tray)  64.3 us
    scatter-add x3, other arithmetic, place_rows(): placed = jax.ops.segment_sum(tile_out, rows_slot, num_segments=row_tiles)  32.6 us
  transfers between devices with their start and end apart: 50, of which 28 were waited for; matrix products, arithmetic and copies ran while one was open for 4% of the time, Pallas kernels for 0%

profile of v1, /device:TPU:2, one launch (start us, length us, event | category | flops | bytes accessed | tf_op | source)
XLA Modules:
  0.0 1106.8 jit_solution(3525400662346640316)
XLA Ops:
  9.1 5.3 collective-permute-start.1
  19.4 3.0 collective-permute-start.3
  29.4 3.0 collective-permute-start.7
  34.5 3.0 collective-permute-start.9
  50.2 3.5 collective-permute-done.14
  56.0 3.2 gather_fusion
  61.7 3.6 convolution_bitcast_fusion.2
  65.3 5.6 copy.84
  70.9 10.7 scatter_custom_fusion
  87.0 78.2 %reduce-scatter.4.cloned.1.call-done = bf16[256,128]{0,1:T(8,128)(2,1)} async-done(((bf16[4096,128]{0,1:T(8,128)(2,1)}), bf16[256,128]{0,1:T(8,128)(2,1)}) %reduce-scatter.4.cloned.1.call-update) | async-done | bytes 65552 | tf_op jit(solution)/shard_map/reduce_scatter | solution.py:64
  167.2 241.6 %all-reduce.3.cloned.1.call-done = f32[128,128]{0,1:T(8,128)} async-done(((f32[128,128]{0,1:T(8,128)}), f32[128,128]{0,1:T(8,128)}) %all-reduce.3.cloned.1.call-update) | async-done | bytes 65552 | tf_op jit(solution)/shard_map/psum | solution.py:75
  410.0 74.2 %psum.29 = f32[128]{0:T(128)S(1)} all-reduce(f32[128]{0:T(128)S(1)} %get-tuple-element.3), channel_id=1, replica_groups=mesh['row'=16,'col'=16] {'row','col'}, use_global_device_ids=true, to_apply=%region_4.6 | all-reduce | flops 128 | bytes 1024 | tf_op jit(solution)/shard_map/psum | solution.py:77
  490.8 3.0 collective-permute-start.18
  500.8 3.0 collective-permute-start.22
  505.9 3.0 collective-permute-start.24
  521.6 3.5 collective-permute-done.29
  527.4 3.2 gather_fusion.1
  533.1 3.6 convolution_bitcast_fusion.1
  536.7 5.6 copy.104
  542.3 10.9 scatter_custom_fusion.1
  559.4 72.7 %reduce-scatter.6.cloned.1.call-done = bf16[256,128]{0,1:T(8,128)(2,1)} async-done(((bf16[4096,128]{0,1:T(8,128)(2,1)}), bf16[256,128]{0,1:T(8,128)(2,1)}) %reduce-scatter.6.cloned.1.call-update) | async-done | bytes 65552 | tf_op jit(solution)/shard_map/reduce_scatter | solution.py:64
  635.4 238.7 %all-reduce.5.cloned.1.call-done = f32[128,128]{0,1:T(8,128)} async-done(((f32[128,128]{0,1:T(8,128)}), f32[128,128]{0,1:T(8,128)}) %all-reduce.5.cloned.1.call-update) | async-done | bytes 65552 | tf_op jit(solution)/shard_map/psum | solution.py:75
  875.4 74.5 %psum.31 = f32[128]{0:T(128)S(1)} all-reduce(f32[128]{0:T(128)S(1)} %get-tuple-element.5), channel_id=1, replica_groups=mesh['row'=16,'col'=16] {'row','col'}, use_global_device_ids=true, to_apply=%region_9.11 | all-reduce | flops 128 | bytes 1024 | tf_op jit(solution)/shard_map/psum | solution.py:77
  950.3 3.0 collective-permute-start.31
  956.1 3.0 collective-permute-start.33
  971.2 3.0 collective-permute-start.39
  987.0 3.5 collective-permute-done.44
  992.7 3.2 gather_fusion.2
  998.4 3.6 convolution_bitcast_fusion
  1002.1 5.6 copy.126
  1007.7 11.0 scatter_custom_fusion.2
  1026.1 71.4 %reduce-scatter.8.cloned.1.call-done = bf16[256,128]{0,1:T(8,128)(2,1)} async-done(((bf16[4096,128]{0,1:T(8,128)(2,1)}), bf16[256,128]{0,1:T(8,128)(2,1)}) %reduce-scatter.8.cloned.1.call-update) | async-done | bytes 65552 | tf_op jit(solution)/shard_map/reduce_scatter | solution.py:64
  (260 shorter events, 127.1 us)
Async XLA Ops:
  7.2 158.1 %reduce-scatter.4.cloned.1.call-start = ((), (), s32[]{:S(2)}) async-start(), calls=%async_computation.3 | async-start | bytes 1114112 | tf_op jit(solution)/shard_map/reduce_scatter | solution.py:64
  9.1 9.4 collective-permute-start
  9.1 10.2 collective-permute-start.1
  18.6 4.9 collective-permute-start.2
  19.4 4.9 collective-permute-start.3
  23.6 4.9 collective-permute-start.4
  28.7 4.9 collective-permute-start.6
  33.7 4.9 collective-permute-start.8
  34.5 4.9 collective-permute-start.9
  38.7 4.9 collective-permute-start.10
  43.8 4.9 collective-permute-start.12
  48.8 4.9 collective-permute-start.14
  87.0 321.8 %all-reduce.3.cloned.1.call-start = ((), (), s32[]{:S(2)}) async-start(), calls=%async_computation.4 | async-start | bytes 131072 | tf_op jit(solution)/shard_map/psum | solution.py:75
  167.0 465.1 %reduce-scatter.6.cloned.1.call-start = ((), (), s32[]{:S(2)}) async-start(), calls=%async_computation.5 | async-start | bytes 1114112 | tf_op jit(solution)/shard_map/reduce_scatter | solution.py:64
  485.0 4.9 collective-permute-start.15
  485.0 5.7 collective-permute-start.16
  490.0 4.9 collective-permute-start.17
  490.8 4.9 collective-permute-start.18
  495.0 4.9 collective-permute-start.19
  500.1 4.9 collective-permute-start.21
  505.9 4.9 collective-permute-start.24
  510.1 4.9 collective-permute-start.25
  520.2 4.9 collective-permute-start.29
  558.6 315.6 %all-reduce.5.cloned.1.call-start = ((), (), s32[]{:S(2)}) async-start(), calls=%async_computation.6 | async-start | bytes 131072 | tf_op jit(solution)/shard_map/psum | solution.py:75
  635.4 462.1 %reduce-scatter.8.cloned.1.call-start = ((), (), s32[]{:S(2)}) async-start(), calls=%async_computation.7 | async-start | bytes 1114112 | tf_op jit(solution)/shard_map/reduce_scatter | solution.py:64
  950.3 5.7 collective-permute-start.31
  956.1 4.9 collective-permute-start.33
  960.4 4.9 collective-permute-start.34
  965.4 4.9 collective-permute-start.36
  971.2 4.9 collective-permute-start.39
  975.5 4.9 collective-permute-start.40
  980.5 4.9 collective-permute-start.42
  (34 other events, 1272.5 us)
Sparse Core Ops, SparseCore 0:
  87.1 78.0 reduce-scatter.3
  172.2 236.5 all-reduce.2
  558.7 73.3 reduce-scatter.5
  637.4 236.6 all-reduce.4
  1024.2 73.2 reduce-scatter.7
